TPU v7x, 512 devices: a whole 4x4x16 slice. The times are simulated.
512 devices in a mesh: frow: 16 (over z_lo, y), fcol: 32 (over z_hi, x, core).
Axes of the slice: x: 4, y: 4, z: 16 (z_hi: 4, z_lo: 4; z = z_hi * 4 + z_lo), core: 2. Of those that a mesh axis runs over, the one named last changes fastest.
Arguments:
- vis: float32 [2, 131072], P(None, ('frow', 'fcol')), may hold values from -6 to 6
- station_pairs: int32 [2, 131072], P(None, ('frow', 'fcol')), may hold values from 0 to 511
- visibility_time_slot: int32 [131072], P(('frow', 'fcol')), may hold values from 0 to 15
- station_u_cells: int32 [512], replicated, may hold values from -4096 to 4095
- station_v_cells: int32 [512], replicated, may hold values from -4096 to 4095
- facet_station_gains: float32 [16, 32, 2, 8192], P('frow', 'fcol'), may hold values from -6 to 6
- holder_device_order: int32 [512], replicated, may hold values from 0 to 511, each once
Outputs:
- image: float32 [16384, 16384], P('frow', 'fcol')
Inputs may be any that keep to these rules, and one draw needn't show every extreme that they name: `holder_device_order`: a permutation; its first 4 entries name distinct devices.
All inputs are finite; a program needn't handle non-finite values.
Results may differ from a plain program's by a relative error of at most 0.0037.
Values sent between devices are 32-bit elements; how exact they have to be, the bound alone decides.
A program may use at most 64 MiB of HBM per device.

v0:
```python
import math
import jax
import jax.numpy as jnp
from jax import lax
from jax.sharding import PartitionSpec as P

R = 1024
C = 512
M = 64
NT = 16
NBLK = 4


def extended_2(x, sides, width):
    for axis, dim in sides:
        size, length = (lax.axis_size(axis), x.shape[dim])
        up = [(i, (i + 1) % size) for i in range(size - 1)]
        down = [(j, i) for i, j in up]
        last = lax.slice_in_dim(x, length - width, length, axis=dim)
        leading = lax.slice_in_dim(x, 0, width, axis=dim)
        before = lax.ppermute(last, axis, up)
        after = lax.ppermute(leading, axis, down)
        x = jnp.concatenate([before, x, after], axis=dim)
    return x


def broadcast(value, axis, source):
    kept = jnp.where(lax.axis_index(axis) == source, value, 0).astype(value.dtype)
    return lax.psum(kept, axis)


def taper_line(length):
    index = jnp.arange(length + 2 * M, dtype=jnp.int32).astype(jnp.float32)
    rising = (index + 0.5) / (2.0 * M)
    falling = (length + 2 * M - index - 0.5) / (2.0 * M)
    return jnp.minimum(jnp.minimum(rising, falling), 1.0)


def phase_angles(freq, pixels, modulus):
    cells = jnp.mod(freq, modulus)[None, :] * jnp.mod(pixels, modulus)[:, None] % modulus
    return cells.astype(jnp.float32) * (2.0 * math.pi / modulus)


def block_weights(values, label_names, g_tab, scale):
    first = label_names[0] * NT + label_names[2]
    second = label_names[1] * NT + label_names[2]
    g1r = g_tab[0][first]
    g1i = g_tab[1][first]
    g2r = g_tab[0][second]
    g2i = g_tab[1][second]
    real_gain = g1r * g2r + g1i * g2i
    imag_gain = g1i * g2r - g1r * g2i
    wreal = scale * (values[0] * real_gain - values[1] * imag_gain)
    wimag = scale * (values[0] * imag_gain + values[1] * real_gain)
    return (wreal, wimag)


def fold_columns(field):
    edges = jnp.concatenate([field[:, :M], field[:, -M:]], 1)
    extended = extended_2(edges, (("fcol", 1),), M)
    inner = field[:, M:-M]
    return jnp.concatenate(
        [inner[:, :M] + extended[:, :M], inner[:, M:-M], inner[:, -M:] + extended[:, -M:]], 1
    )


def fold_rows(field):
    edges = jnp.concatenate([field[:M], field[-M:]], 0)
    extended = extended_2(edges, (("frow", 0),), M)
    inner = field[M:-M]
    return jnp.concatenate([inner[:M] + extended[:M], inner[M:-M], inner[-M:] + extended[-M:]], 0)


def shards(
    vis,
    station_pairs,
    visibility_time_slot,
    station_u_cells,
    station_v_cells,
    facet_station_gains,
    holder_device_order,
):
    count_rows = lax.axis_size("frow")
    count_cols = lax.axis_size("fcol")
    n_rows = R * count_rows
    n_cols = C * count_cols
    frow_at = lax.axis_index("frow")
    fcol_at = lax.axis_index("fcol")
    g_tab = facet_station_gains[0, 0]
    label_names = jnp.concatenate([station_pairs, visibility_time_slot[None, :]], 0)
    block_size = vis.shape[1]
    scale = 0.5 / math.sqrt(NBLK * block_size)
    rows = frow_at * R - M + jnp.arange(R + 2 * M, dtype=jnp.int32)
    cols = fcol_at * C - M + jnp.arange(C + 2 * M, dtype=jnp.int32)
    total = jnp.zeros((R + 2 * M, C + 2 * M), jnp.float32)
    for step in range(NBLK):
        owner = holder_device_order[step]
        values, tag_names = (
            broadcast(vis, ("frow", "fcol"), owner),
            broadcast(label_names, ("frow", "fcol"), owner),
        )
        wreal, wimag = block_weights(values, tag_names, g_tab, scale)
        frequency_u = station_u_cells[tag_names[0]] - station_u_cells[tag_names[1]]
        frequency_v = station_v_cells[tag_names[0]] - station_v_cells[tag_names[1]]
        theta = phase_angles(frequency_u, rows, n_rows)
        phi = phase_angles(frequency_v, cols, n_cols).T
        row_table = jnp.concatenate([jnp.cos(theta), jnp.sin(theta)], 1).astype(jnp.bfloat16)
        top = wreal[:, None] * jnp.cos(phi) - wimag[:, None] * jnp.sin(phi)
        bottom = -(wimag[:, None] * jnp.cos(phi) + wreal[:, None] * jnp.sin(phi))
        col_table = jnp.concatenate([top, bottom], 0).astype(jnp.bfloat16)
        total = total + jnp.dot(row_table, col_table, preferred_element_type=jnp.float32)
    tapered = total * taper_line(R)[:, None] * taper_line(C)[None, :]
    image = fold_rows(fold_columns(tapered))
    return image


def solution(mesh):
    return jax.shard_map(
        shards,
        mesh=mesh,
        in_specs=(
            P(None, ("frow", "fcol")),
            P(None, ("frow", "fcol")),
            P(("frow", "fcol")),
            P(),
            P(),
            P("frow", "fcol", None, None),
            P(),
        ),
        out_specs=P("frow", "fcol"),
        check_vma=False,
    )
```

profile of v0, /device:TPU:71, one launch (start us, length us, event | category | flops | bytes accessed | tf_op | source)
XLA Modules:
  0.0 365.5 jit_solution(12329082438858966034)
XLA Ops:
  4.7 105.5 %all-reduce = (s32[3,256]{1,0:T(4,128)S(1)}, s32[3,256]{1,0:T(4,128)S(1)}, s32[3,256]{1,0:T(4,128)S(1)}, s32[3,256]{1,0:T(4,128)S(1)}) all-reduce(s32[3,256]{1,0:T(4,128)S(1)} %get-tuple-element.78, s32[3,256]{1,0:T(4,128)S(1)} %get-tuple-element.76, ...), channel_id=1, replica_groups=mesh['frow'=16,'fcol'=32] {'frow','fcol'}, use_global_device_ids=true, to_apply=%region_0.1 | all-reduce | flops 3072 | bytes 24576 | tf_op jit(solution)/shard_map/psum | solution.py:29
  139.1 1.9 gather_fusion.6
  141.1 1.9 gather_fusion.7
  143.0 1.9 gather_fusion
  145.0 1.9 gather_fusion.1
  147.0 1.9 gather_fusion.22
  148.9 1.9 gather_fusion.16
  150.9 1.9 gather_fusion.23
  152.8 1.9 gather_fusion.17
  154.8 1.9 gather_fusion.14
  156.8 1.9 gather_fusion.8
  158.7 1.9 gather_fusion.15
  160.7 1.9 gather_fusion.9
  162.6 1.9 gather_fusion.30
  166.6 1.9 gather_fusion.31
  168.5 1.9 gather_fusion.25
  170.6 99.6 %all-reduce.1 = (f32[2,256]{1,0:T(2,128)S(1)}, f32[2,256]{1,0:T(2,128)S(1)}, f32[2,256]{1,0:T(2,128)S(1)}, f32[2,256]{1,0:T(2,128)S(1)}) all-reduce(f32[2,256]{1,0:T(2,128)S(1)} %get-tuple-element.89, f32[2,256]{1,0:T(2,128)S(1)} %get-tuple-element.88, ...), channel_id=1, replica_groups=mesh['frow'=16,'fcol'=32] {'frow','fcol'}, use_global_device_ids=true, to_apply=%region_1.2 | all-reduce | flops 2048 | bytes 16384 | tf_op jit(solution)/shard_map/psum | solution.py:29
  270.5 19.1 %cosine_convert_fusion = (bf16[1152,256]{1,0:T(8,128)(2,1)S(1)}, bf16[1152,256]{1,0:T(8,128)(2,1)S(1)}, bf16[1152,256]{1,0:T(8,128)(2,1)S(1)}, bf16[1152,256]{1,...) fusion(s32[1152]{0:T(1024)S(1)} %add_select_fusion.8, ...), kind=kLoop, calls=%fused_computation.97 | loop fusion | flops 18874368 | bytes 4727296 | tf_op jit(solution)/shard_map/convert.2
  289.6 11.5 %subtract_convert_fusion = (bf16[256,640]{1,0:T(8,128)(2,1)S(1)}, bf16[256,640]{1,0:T(8,128)(2,1)S(1)}, bf16[256,640]{1,0:T(8,128)(2,1)S(1)}, bf16[256,640]{1,0:...) fusion(f32[256]{0:T(256)S(1)} %add_multiply_fusion, ...), kind=kLoop, calls=%fused_computation.137 | loop fusion | flops 15073280 | bytes 2636288 | tf_op jit(solution)/shard_map/convert
  305.5 6.8 %collective-permute-start = (f32[1152,64]{0,1:T(8,128)S(1)}, f32[1152,64]{0,1:T(8,128)S(1)}, u32[]{:S(2)}, u32[]{:S(2)}) collective-permute-start(f32[1152,64]{0,1:T(8,128)S(1)} %slice.281), channel_id=1, source_target_pairs={{0,1},{1,2},{2,3},{3,4},{4,5},{5,6},{6,7},{7,8},{8,9},{9,10},{10,1... | collective-permute-start | bytes 884744 | tf_op jit(solution)/shard_map/ppermute | solution.py:21
  312.3 10.0 %collective-permute-done = f32[1152,64]{0,1:T(8,128)S(1)} collective-permute-done((f32[1152,64]{0,1:T(8,128)S(1)}, f32[1152,64]{0,1:T(8,128)S(1)}, u32[]{:S(2)}, u32[]{:S(2)}) %collective-permute-start) | collective-permute-done | bytes 294944 | tf_op jit(solution)/shard_map/ppermute | solution.py:21
  324.4 20.4 %collective-permute-done.1 = f32[1152,64]{0,1:T(8,128)S(1)} collective-permute-done((f32[1152,64]{0,1:T(8,128)S(1)}, f32[1152,64]{0,1:T(8,128)S(1)}, u32[]{:S(2)}, u32[]{:S(2)}) %collective-permute-start.1) | collective-permute-done | bytes 294944 | tf_op jit(solution)/shard_map/ppermute | solution.py:22
  347.0 7.3 %collective-permute-done.2 = f32[64,512]{0,1:T(8,128)S(1)} collective-permute-done((f32[64,512]{0,1:T(8,128)S(1)}, f32[64,512]{0,1:T(8,128)S(1)}, u32[]{:S(2)}, u32[]{:S(2)}) %collective-permute-start.2) | collective-permute-done | bytes 131104 | tf_op jit(solution)/shard_map/ppermute | solution.py:21
  358.0 3.6 collective-permute-done.3
  (88 shorter events, 49.3 us)
Async XLA Ops:
  0.0 139.1 %copy-start = (s32[512]{0:T(512)S(1)}, s32[512]{0:T(512)}, u32[]{:S(2)}) copy-start(s32[512]{0:T(512)} %param.11) | copy-start | bytes 6148
  139.1 4.0 %copy-start.1 = (s32[512]{0:T(512)S(1)}, s32[512]{0:T(512)}, u32[]{:S(2)}) copy-start(s32[512]{0:T(512)} %param.10) | copy-start | bytes 6148
  166.6 4.0 %copy-start.3 = (f32[2,256]{1,0:T(2,128)S(1)}, f32[2,256]{1,0:T(2,128)}, u32[]{:S(2)}) copy-start(f32[2,256]{1,0:T(2,128)} %param.7) | copy-start | bytes 6148
  305.5 16.8 %collective-permute-start = (f32[1152,64]{0,1:T(8,128)S(1)}, f32[1152,64]{0,1:T(8,128)S(1)}, u32[]{:S(2)}, u32[]{:S(2)}) collective-permute-start(f32[1152,64]{0,1:T(8,128)S(1)} %slice.281), channel_id=1, source_target_pairs={{0,1},{1,2},{2,3},{3,4},{4,5},{5,6},{6,7},{7,8},{8,9},{9,10},{10,1... | collective-permute-start | bytes 884744 | tf_op jit(solution)/shard_map/ppermute | solution.py:21
  322.4 22.5 %collective-permute-start.1 = (f32[1152,64]{0,1:T(8,128)S(1)}, f32[1152,64]{0,1:T(8,128)S(1)}, u32[]{:S(2)}, u32[]{:S(2)}) collective-permute-start(f32[1152,64]{0,1:T(8,128)S(1)} %get-tuple-element.26), channel_id=1, source_target_pairs={{1,0},{2,1},{3,2},{4,3},{5,4},{6,5},{7,6},{8,7},{9,8},{10,9},{11,1... | collective-permute-start | bytes 884744 | tf_op jit(solution)/shard_map/ppermute | solution.py:22
  345.1 9.2 %collective-permute-start.2 = (f32[64,512]{0,1:T(8,128)S(1)}, f32[64,512]{0,1:T(8,128)S(1)}, u32[]{:S(2)}, u32[]{:S(2)}) collective-permute-start(f32[64,512]{0,1:T(8,128)S(1)} %pad_maximum_fusion.3), channel_id=1, source_target_pairs={{0,32},{32,64},{64,96},{96,128},{128,160},{160,192},{192,224},{224... | collective-permute-start | bytes 393224 | tf_op jit(solution)/shard_map/ppermute | solution.py:21
  354.4 7.1 %collective-permute-start.3 = (f32[64,512]{0,1:T(8,128)S(1)}, f32[64,512]{0,1:T(8,128)S(1)}, u32[]{:S(2)}, u32[]{:S(2)}) collective-permute-start(f32[64,512]{0,1:T(8,128)S(1)} %get-tuple-element.28), channel_id=1, source_target_pairs={{32,0},{64,32},{96,64},{128,96},{160,128},{192,160},{224,192},{256... | collective-permute-start | bytes 393224 | tf_op jit(solution)/shard_map/ppermute | solution.py:22
  356.5 1.4 copy-start.2
  361.5 1.5 slice-start
where the time goes:
time: 366 us
  blocking collectives  205 us (56%)
  local copies, waits for them, and re-layouts  66 us (18%)
  waiting for transfers between devices  41.3 us (11%)
  other arithmetic  32.8 us (9%)
  starting transfers between devices  12.6 us (3%)
  matrix products  4.44 us (1%)
    psum x2, blocking collectives, broadcast(): return lax.psum(kept, axis)  205 us
    another operation x2, other arithmetic  30.5 us
    ppermute x2, waiting for transfers between devices, extended_2(): after = lax.ppermute(leading, axis, down)  24 us
    ppermute x2, waiting for transfers between devices, extended_2(): before = lax.ppermute(last, axis, up)  17.3 us
    gather x8, local copies, waits for them, and re-layouts, shards(): frequency_v = station_v_cells[tag_names[0]] - station_v_cells[tag_names[1]]  15.6 us
    gather x8, local copies, waits for them, and re-layouts, shards(): frequency_u = station_u_cells[tag_names[0]] - station_u_cells[tag_names[1]]  15.6 us
    ppermute x2, starting transfers between devices, extended_2(): before = lax.ppermute(last, axis, up)  8.72 us
  transfers between devices with their start and end apart: 4, of which 4 were waited for; matrix products, arithmetic and copies ran while one was open for 0% of the time, Pallas kernels for 0%

commit v1 on v0

--- a/solution.py
+++ b/solution.py
@@ -25,8 +25,13 @@
 
 
 def broadcast(value, axis, source):
+
+    def mix_the_local_data(message, chip_axis):
+        near = jnp.sum(lax.all_gather(message, axis_name=chip_axis), axis=0)
+        return near
+
     kept = jnp.where(lax.axis_index(axis) == source, value, 0).astype(value.dtype)
-    return lax.psum(kept, axis)
+    return mix_the_local_data(kept, axis)
 
 
 def taper_line(length):

time: 366 us -> 6250 us (17.08)
  waiting for transfers between devices: 41.3 us -> 6100 us
  blocking collectives: 205 us -> 0 us
    all_gather x0 -> x8, waiting for transfers between devices: none -> 6050 us  [mix_the_local_data(): near = jnp.sum(lax.all_gather(message, axis_name=chip_axis), axis=0)]
    psum x2 -> x0, blocking collectives: 205 us -> none  [broadcast(): return lax.psum(kept, axis)]
  transfers between devices with their start and end apart: 4 -> 12, of which waited for: 4 -> 12; matrix products, arithmetic and copies ran while one was open for 0% -> 1% of each run, Pallas kernels for 0% -> 0%
where the time goes in v1:
time: 6250 us
  waiting for transfers between devices  6100 us (98%)
  local copies, waits for them, and re-layouts  66.4 us (1%)
    all_gather x8, waiting for transfers between devices, mix_the_local_data(): near = jnp.sum(lax.all_gather(message, axis_name=chip_axis), axis=0)  6050 us
  transfers between devices with their start and end apart: 12, of which 12 were waited for; matrix products, arithmetic and copies ran while one was open for 1% of the time, Pallas kernels for 0%

profile of v1, /device:TPU:71, one launch (start us, length us, event | category | flops | bytes accessed | tf_op | source)
XLA Modules:
  0.0 6250.2 jit_solution(1130338181479251925)
XLA Ops:
  18.5 760.6 %all-gather.29.cloned.1.call-done = f32[512,2,256]{2,1,0:T(2,128)} async-done(((f32[1,2,256]{2,1,0:T(2,128)}), f32[512,2,256]{2,1,0:T(2,128)}) %all-gather.29.cloned.1.call-update) | async-done | bytes 1048592 | tf_op jit(solution)/shard_map/all_gather | solution.py:30
  780.9 758.4 %all-gather.31.cloned.1.call-done = f32[512,2,256]{2,1,0:T(2,128)} async-done(((f32[1,2,256]{2,1,0:T(2,128)}), f32[512,2,256]{2,1,0:T(2,128)}) %all-gather.31.cloned.1.call-update) | async-done | bytes 1048592 | tf_op jit(solution)/shard_map/all_gather | solution.py:30
  1541.0 758.4 %all-gather.27.cloned.1.call-done = f32[512,2,256]{2,1,0:T(2,128)} async-done(((f32[1,2,256]{2,1,0:T(2,128)}), f32[512,2,256]{2,1,0:T(2,128)}) %all-gather.27.cloned.1.call-update) | async-done | bytes 1048592 | tf_op jit(solution)/shard_map/all_gather | solution.py:30
  2301.2 758.2 %all-gather.25.cloned.1.call-done = f32[512,2,256]{2,1,0:T(2,128)} async-done(((f32[1,2,256]{2,1,0:T(2,128)}), f32[512,2,256]{2,1,0:T(2,128)}) %all-gather.25.cloned.1.call-update) | async-done | bytes 1048592 | tf_op jit(solution)/shard_map/all_gather | solution.py:30
  3061.3 760.2 %all-gather.21.cloned.1.call-done = s32[512,3,256]{2,1,0:T(4,128)} async-done(((s32[1,3,256]{2,1,0:T(4,128)}), s32[512,3,256]{2,1,0:T(4,128)}) %all-gather.21.cloned.1.call-update) | async-done | bytes 1572880 | tf_op jit(solution)/shard_map/all_gather | solution.py:30
  3821.5 2.1 reduce_sum.76
  3830.7 752.7 %all-gather.23.cloned.1.call-done = s32[512,3,256]{2,1,0:T(4,128)} async-done(((s32[1,3,256]{2,1,0:T(4,128)}), s32[512,3,256]{2,1,0:T(4,128)}) %all-gather.23.cloned.1.call-update) | async-done | bytes 1572880 | tf_op jit(solution)/shard_map/all_gather | solution.py:30
  4583.4 2.1 reduce_sum.78
  4592.5 753.0 %all-gather.19.cloned.1.call-done = s32[512,3,256]{2,1,0:T(4,128)} async-done(((s32[1,3,256]{2,1,0:T(4,128)}), s32[512,3,256]{2,1,0:T(4,128)}) %all-gather.19.cloned.1.call-update) | async-done | bytes 1572880 | tf_op jit(solution)/shard_map/all_gather | solution.py:30
  5345.5 2.1 reduce_sum.74
  5354.6 753.0 %all-gather.17.cloned.1.call-done = s32[512,3,256]{2,1,0:T(4,128)} async-done(((s32[1,3,256]{2,1,0:T(4,128)}), s32[512,3,256]{2,1,0:T(4,128)}) %all-gather.17.cloned.1.call-update) | async-done | bytes 1572880 | tf_op jit(solution)/shard_map/all_gather | solution.py:30
  6107.6 2.1 reduce_sum.72
  6122.6 1.9 gather_fusion.1
  6126.5 1.9 gather_fusion.8
  6130.4 1.9 gather_fusion.9
  6134.4 1.9 gather_fusion.16
  6144.2 2.2 gather_fusion.31
  6148.5 19.1 cosine_convert_fusion
  6167.6 11.5 subtract_convert_fusion
  6183.5 8.2 collective-permute-start
  6191.8 10.1 collective-permute-done
  6204.0 18.8 collective-permute-done.1
  6224.8 7.3 collective-permute-done.2
  6235.8 3.6 collective-permute-done.3
  (114 shorter events, 82.0 us)
Async XLA Ops:
  6.5 6110.2 %copy-start = (s32[512]{0:T(512)S(1)}, s32[512]{0:T(512)}, u32[]{:S(2)}) copy-start(s32[512]{0:T(512)} %param.11) | copy-start | bytes 6148
  6.5 772.5 %all-gather.29.cloned.1.call-start = ((), (), s32[]{:S(2)}) async-start(), calls=%async_computation.6 | async-start | bytes 1050624 | tf_op jit(solution)/shard_map/all_gather | solution.py:30
  11.9 1527.3 %all-gather.31.cloned.1.call-start = ((), (), s32[]{:S(2)}) async-start(), calls=%async_computation.7 | async-start | bytes 1050624 | tf_op jit(solution)/shard_map/all_gather | solution.py:30
  12.6 2286.8 %all-gather.27.cloned.1.call-start = ((), (), s32[]{:S(2)}) async-start(), calls=%async_computation.5 | async-start | bytes 1050624 | tf_op jit(solution)/shard_map/all_gather | solution.py:30
  13.4 3046.1 %all-gather.25.cloned.1.call-start = ((), (), s32[]{:S(2)}) async-start(), calls=%async_computation.4 | async-start | bytes 1050624 | tf_op jit(solution)/shard_map/all_gather | solution.py:30
  14.0 3807.5 %all-gather.21.cloned.1.call-start = ((), (), s32[]{:S(2)}) async-start(), calls=%async_computation.2 | async-start | bytes 2101248 | tf_op jit(solution)/shard_map/all_gather | solution.py:30
  15.3 4568.1 %all-gather.23.cloned.1.call-start = ((), (), s32[]{:S(2)}) async-start(), calls=%async_computation.3 | async-start | bytes 2101248 | tf_op jit(solution)/shard_map/all_gather | solution.py:30
  15.9 5329.6 %all-gather.19.cloned.1.call-start = ((), (), s32[]{:S(2)}) async-start(), calls=%async_computation.1 | async-start | bytes 2101248 | tf_op jit(solution)/shard_map/all_gather | solution.py:30
  16.7 6090.9 %all-gather.17.cloned.1.call-start = ((), (), s32[]{:S(2)}) async-start(), calls=%async_computation | async-start | bytes 2101248 | tf_op jit(solution)/shard_map/all_gather | solution.py:30
  6116.7 4.0 copy-start.1
  6183.5 18.3 collective-permute-start
  6201.9 20.8 collective-permute-start.1
  6222.9 9.2 collective-permute-start.2
  6232.3 7.1 collective-permute-start.3
  6234.4 1.4 copy-start.2
  6239.4 1.5 slice-start
Sparse Core Ops, SparseCore 0:
  12.0 767.0 all-gather.28
  781.2 758.0 all-gather.30
  1541.4 758.0 all-gather.26
  2301.4 758.0 all-gather.24
  3061.4 759.9 all-gather.20
  3823.4 759.9 all-gather.22
  4585.5 759.9 all-gather.18
  5347.6 759.9 all-gather.16
